TPU v7x, 32 devices: a whole 2x2x4 slice. The times are simulated.
32 devices in a mesh: cp: 8 (over y, x, core), sp: 4 (over z).
Axes of the slice: x: 2, y: 2, z: 4, core: 2. Of those that a mesh axis runs over, the one named last changes fastest.
Arguments:
- queries: bfloat16 [3072, 2048], P(('cp', 'sp')), may hold values from -6 to 6
- key_vectors: bfloat16 [3072, 512], P(('cp', 'sp')), may hold values from -6 to 6
- value_matrix: bfloat16 [3072, 512], P(('cp', 'sp')), may hold values from -6 to 6
- span_order: int32 [8], replicated, may hold values from 0 to 7, each once
Outputs:
- attended: bfloat16 [3072, 2048], P(('cp', 'sp'))
Inputs may be any that keep to these rules, and one draw needn't show every extreme that they name: `span_order`: each value appears exactly once.
All inputs are finite; a program needn't handle non-finite values.
Results may differ from a plain program's by a relative error of at most 0.0055.
Values may be sent and summed in bfloat16 or wider, within the bound.
A program may use at most 128 MiB of HBM per device.

v0:
```python
import jax
import jax.numpy as jnp
from jax import lax
from jax.sharding import PartitionSpec as P

HEAD_WIDTH = 128


masked_score = -1e30


def span_position(row_ids, span_order, pair_count, span_rows):
    slot_ids = row_ids // span_rows
    pair_ids = slot_ids // 2
    picked = jnp.sum(
        jnp.where(
            pair_ids[:, None] == jnp.arange(pair_count, dtype=jnp.int32)[None, :],
            span_order[None, :],
            0,
        ),
        axis=1,
    )
    span_ids = jnp.where(slot_ids % 2 == 1, 2 * pair_count - 1 - picked, picked)
    return span_ids * span_rows + row_ids % span_rows


def absorb_block(state_in, query_blk, query_pos, key_blk, value_blk, key_pos):
    run_max, run_sum, accumulated = state_in
    scores = jnp.einsum(
        "qhd,kd->hqk", query_blk, key_blk, preferred_element_type=jnp.float32
    ) * query_blk.shape[2] ** (-0.5)
    allowed = key_pos[None, None, :] <= query_pos[None, :, None]
    new_peak = jnp.maximum(run_max, jnp.max(jnp.where(allowed, scores, masked_score), axis=2))
    weights = jnp.where(allowed, jnp.exp(scores - new_peak[:, :, None]), 0.0)
    factor = jnp.exp(run_max - new_peak)
    run_sum = run_sum * factor + jnp.sum(weights, axis=2)
    accumulated = accumulated * factor[:, :, None] + jnp.einsum(
        "hqk,kd->hqd", weights.astype(jnp.bfloat16), value_blk, preferred_element_type=jnp.float32
    )
    return (new_peak, run_sum, accumulated)


def pick_block(key_count, unit_rows):
    block_row_list = unit_rows
    while block_row_list * 2 <= 1024 and key_count % (block_row_list * 2) == 0:
        block_row_list = block_row_list * 2
    return block_row_list


def guarded(state_in, query_blk, query_pos, key_blk, value_blk, key_pos, lowest):

    def compute(states):
        return absorb_block(states, query_blk, query_pos, key_blk, value_blk, key_pos)

    def unchanged(states):
        return states

    return lax.cond(lowest <= jnp.max(query_pos), compute, unchanged, state_in)


def sweep(carries, query_list, key_rows, value_rows, position_of, block_row_list):
    key_count = key_rows.shape[0]

    def advance(states, offset):
        key_blk = lax.dynamic_slice_in_dim(key_rows, offset, block_row_list, 0)
        value_blk = lax.dynamic_slice_in_dim(value_rows, offset, block_row_list, 0)
        key_pos = position_of(offset + jnp.arange(block_row_list, dtype=jnp.int32))
        lowest = jnp.min(key_pos)
        updated = []
        for state_in, entry in zip(states, query_list):
            updated.append(
                guarded(state_in, entry[0], entry[1], key_blk, value_blk, key_pos, lowest)
            )
        return (tuple(updated), None)

    offsets = jnp.arange(key_count // block_row_list, dtype=jnp.int32) * block_row_list
    return lax.scan(advance, carries, offsets)[0]


def per_device(queries, key_vectors, value_matrix, span_order):
    tok_rows = queries.shape[0]
    cp_count = lax.axis_size("cp")
    sp_count = lax.axis_size("sp")
    local_query = lax.all_to_all(queries, "sp", split_axis=1, concat_axis=0, tiled=True)
    group_rows = local_query.shape[0]
    span_rows = group_rows // 2
    head_count = local_query.shape[1] // HEAD_WIDTH
    query_heads = local_query.reshape(group_rows, head_count, HEAD_WIDTH)
    group_id = lax.axis_index("cp")
    query_ids = group_id * group_rows + jnp.arange(group_rows, dtype=jnp.int32)
    query_pos = span_position(query_ids, span_order, cp_count, span_rows)
    query_list = [(query_heads, query_pos)]
    initial = tuple(
        (
            (
                jnp.full((head_count, entry[1].shape[0]), masked_score, jnp.float32),
                jnp.zeros((head_count, entry[1].shape[0]), jnp.float32),
                jnp.zeros((head_count, entry[1].shape[0], HEAD_WIDTH), jnp.float32),
            )
            for entry in query_list
        )
    )
    whole_key, whole_value = (
        lax.all_gather(key_vectors, "cp", axis=0, tiled=True),
        lax.all_gather(value_matrix, "cp", axis=0, tiled=True),
    )
    head_key, head_value = (
        lax.all_to_all(whole_key, "sp", split_axis=1, concat_axis=0, tiled=True),
        lax.all_to_all(whole_value, "sp", split_axis=1, concat_axis=0, tiled=True),
    )
    total_rows = head_key.shape[0]
    span_count = total_rows // span_rows
    slot_ids = jnp.arange(span_count, dtype=jnp.int32)
    pair_pick = jnp.sum(
        jnp.where(
            (slot_ids // 2)[:, None] == jnp.arange(cp_count, dtype=jnp.int32)[None, :],
            span_order[None, :],
            0,
        ),
        axis=1,
    )
    span_of_slot = jnp.where(slot_ids % 2 == 1, 2 * cp_count - 1 - pair_pick, pair_pick)
    slot_of_span = jnp.sum(
        jnp.where(span_of_slot[None, :] == slot_ids[:, None], slot_ids[None, :], 0), axis=1
    )

    def position_layout(rows):
        stored = jnp.transpose(rows.reshape(sp_count, cp_count, tok_rows, HEAD_WIDTH), (1, 0, 2, 3))
        spans = stored.reshape(span_count, span_rows, HEAD_WIDTH)
        return jnp.take(spans, slot_of_span, axis=0).reshape(total_rows, HEAD_WIDTH)

    ordered_key = position_layout(head_key)
    ordered_value = position_layout(head_value)

    def plain_position(row_ids):
        return row_ids

    carries = sweep(
        initial,
        query_list,
        ordered_key,
        ordered_value,
        plain_position,
        pick_block(total_rows, span_rows),
    )
    pieces = [entry[2] / entry[1][:, :, None] for entry in carries]
    joined = pieces[0]
    mixed_rows = (
        jnp.transpose(joined, (1, 0, 2))
        .reshape(group_rows, head_count * HEAD_WIDTH)
        .astype(jnp.bfloat16)
    )
    return lax.all_to_all(mixed_rows, "sp", split_axis=0, concat_axis=1, tiled=True)


def solution(mesh):
    return jax.shard_map(
        per_device,
        mesh=mesh,
        in_specs=(P(("cp", "sp"), None), P(("cp", "sp"), None), P(("cp", "sp"), None), P()),
        out_specs=P(("cp", "sp"), None),
        check_vma=False,
    )
```

profile of v0, /device:TPU:0, one launch (start us, length us, event | category | flops | bytes accessed | tf_op | source)
XLA Modules:
  0.0 125.0 jit_solution(15922890918576906589)
XLA Ops:
  0.0 0.0 copy-start
  0.0 0.0 copy-start.1
  0.0 1.8 %copy.54 = bf16[12,4,8,512]{3,2,0,1:T(8,128)(2,1)} copy(bf16[12,4,8,512]{3,2,1,0:T(8,128)(2,1)} %bitcast.62) | data formatting | bytes 786432 | tf_op jit(solution)/shard_map/all_to_all | solution.py:84
  1.8 6.3 %all-to-all-start.1 = ((bf16[96,4,512]{2,0,1:T(8,128)(2,1)}), bf16[96,4,512]{2,0,1:T(8,128)(2,1)S(1)}, u32[]{:S(2)}, u32[]{:S(2)}) async-start(bf16[96,4,512]{2,0,1:T(8,128)(2,1)} %bitcast.49), calls=%async_computation.1 | async-start | bytes 786432 | tf_op jit(solution)/shard_map/all_to_all | solution.py:84
  8.2 10.7 %all_gather.6 = bf16[768,512]{1,0:T(8,128)(2,1)S(1)} all-gather(bf16[96,512]{1,0:T(8,128)(2,1)} %param.11), channel_id=1, replica_groups=mesh['cp'=8,'sp'=4] {'cp'}, dimensions={0}, use_global_device_ids=true | all-gather | bytes 884736 | tf_op jit(solution)/shard_map/all_gather | solution.py:104
  18.9 1.2 copy.40
  20.1 0.0 all-to-all-done.1
  20.1 5.1 %all-to-all-start = ((bf16[768,4,128]{0,2,1:T(8,128)(2,1)}), bf16[768,4,128]{0,2,1:T(8,128)(2,1)S(1)}, u32[]{:S(2)}, u32[]{:S(2)}) async-start(bf16[768,4,128]{0,2,1:T(8,128)(2,1)} %bitcast.4), calls=%async_computation | async-start | bytes 1572864 | tf_op jit(solution)/shard_map/all_to_all | solution.py:108
  25.2 0.0 copy-done
  25.2 10.0 %all_gather.7 = bf16[768,512]{1,0:T(8,128)(2,1)S(1)} all-gather(bf16[96,512]{1,0:T(8,128)(2,1)S(1)} %copy-done), channel_id=1, replica_groups=mesh['cp'=8,'sp'=4] {'cp'}, dimensions={0}, use_global_device_ids=true | all-gather | bytes 884736 | tf_op jit(solution)/shard_map/all_gather | solution.py:105
  35.2 1.2 copy.44
  36.4 0.0 copy-done.1
  36.4 0.1 select_reduce_fusion.2
  36.5 9.3 %all-to-all-done = bf16[768,4,128]{0,2,1:T(8,128)(2,1)S(1)} async-done(((bf16[768,4,128]{0,2,1:T(8,128)(2,1)}), bf16[768,4,128]{0,2,1:T(8,128)(2,1)S(1)}, u32[]{:S(2)}, u32[]{:S(2)}) %all-to-all-start) | async-done | bytes 786464 | tf_op jit(solution)/shard_map/all_to_all | solution.py:108
  45.8 3.5 %all-to-all-start.2 = ((bf16[768,4,128]{0,2,1:T(8,128)(2,1)}), bf16[768,4,128]{0,2,1:T(8,128)(2,1)S(1)}, u32[]{:S(2)}, u32[]{:S(2)}) async-start(bf16[768,4,128]{0,2,1:T(8,128)(2,1)} %bitcast.11), calls=%async_computation.2 | async-start | bytes 1572864 | tf_op jit(solution)/shard_map/all_to_all | solution.py:109
  49.3 0.1 select_reduce_fusion.1
  49.5 0.1 select_reduce_fusion
  49.5 0.7 fusion.31
  50.3 0.1 reshape.137
  50.4 0.1 copy.47
  50.4 0.4 copy.41
  50.8 0.1 copy.42
  50.9 18.2 %all-to-all-done.2 = bf16[768,4,128]{0,2,1:T(8,128)(2,1)S(1)} async-done(((bf16[768,4,128]{0,2,1:T(8,128)(2,1)}), bf16[768,4,128]{0,2,1:T(8,128)(2,1)S(1)}, u32[]{:S(2)}, u32[]{:S(2)}) %all-to-all-start.2) | async-done | bytes 786464 | tf_op jit(solution)/shard_map/all_to_all | solution.py:109
  69.0 0.4 copy.45
  69.4 0.1 copy.46
  69.5 0.7 gather_fusion
  70.2 0.7 gather_fusion.1
  70.9 1.1 broadcast_select_fusion
  72.0 0.1 broadcast_in_dim.98
  72.1 37.8 %while.15 = (s32[]{:T(128)}, f32[4,384]{1,0:T(4,128)S(1)}, f32[4,384]{1,0:T(4,128)S(1)}, f32[4,384,128]{2,1,0:T(8,128)S(1)}, s32[4]{0:T(128)S(1)}, /*index=5*/s3...) while((s32[]{:T(128)}, f32[4,384]{1,0:T(4,128)S(1)}, ...), condition=%wide.region_10.12_spmd, body=%wide.region_4.11_spmd.sunk | while | flops 617648640 | bytes 17801024 | solution.py:77
  72.1 0.6 dynamic_slice.36
  72.6 1.2 iota_add_fusion.3
  75.1 6.4 %conditional.2 = ((f32[4,384]{1,0:T(4,128)S(1)}, f32[4,384]{1,0:T(4,128)S(1)}, f32[4,384,128]{2,1,0:T(8,128)S(1)})) conditional(s32[]{:T(128)} %convert_element_type.31, (f32[4,384]{1,0:T(4,128)S(1)}, f32[4,384]{1,0:T(4,128)S(1)}, f32[4,384,128]{2,1,0:T(8,128)S(1)}) %tuple.53, (s32[768]{0:T(1024)S(1)}, s32[384]{0:T(512)S(1)}, s32[]{:T(128)}, ...), branch_computations={%region_6.7_spmd, %region_7.10_spmd} | conditional | flops 617647104 | bytes 17797706 | solution.py:58
  76.8 0.2 broadcast_compare_fusion
  77.0 1.0 fusion
  78.0 1.0 fusion.4
  79.0 2.5 %fusion.8 = f32[4,384,128]{2,1,0:T(8,128)S(1)} fusion(f32[768,384,4]{1,0,2:T(8,128)S(1)} %get-tuple-element.282, f32[4,384]{1,0:T(4,128)S(1)} %max.5, pred[384,768]{0,1:T(8,128)(4,1)S(1)} %broadcast_compare_fusion, f32[4,384,128]{2,1,0:T(8,128)S(1)} %get-tuple-element.187, f32[4,384]{1,0:T(4,128)S(1)} %get-tuple-element.278, ...), kind=kOutput, calls=%fused_computation.11 | convolution fusion | flops 307101696 | bytes 6795268 | tf_op jit(solution)/shard_map/while/body/eval_jaxpr/cond/branch_1_fun/hqk,kd->hqd/dot_general | solution.py:37
  81.5 0.6 dynamic_slice.36
  82.1 1.2 iota_add_fusion.3
  84.5 6.4 %conditional.2 = ((f32[4,384]{1,0:T(4,128)S(1)}, f32[4,384]{1,0:T(4,128)S(1)}, f32[4,384,128]{2,1,0:T(8,128)S(1)})) conditional(s32[]{:T(128)} %convert_element_type.31, (f32[4,384]{1,0:T(4,128)S(1)}, f32[4,384]{1,0:T(4,128)S(1)}, f32[4,384,128]{2,1,0:T(8,128)S(1)}) %tuple.53, (s32[768]{0:T(1024)S(1)}, s32[384]{0:T(512)S(1)}, s32[]{:T(128)}, ...), branch_computations={%region_6.7_spmd, %region_7.10_spmd} | conditional | flops 617647104 | bytes 17797706 | solution.py:58
  86.2 0.2 broadcast_compare_fusion
  86.4 1.0 fusion
  87.4 1.0 fusion.4
  88.4 2.5 %fusion.8 = f32[4,384,128]{2,1,0:T(8,128)S(1)} fusion(f32[768,384,4]{1,0,2:T(8,128)S(1)} %get-tuple-element.282, f32[4,384]{1,0:T(4,128)S(1)} %max.5, pred[384,768]{0,1:T(8,128)(4,1)S(1)} %broadcast_compare_fusion, f32[4,384,128]{2,1,0:T(8,128)S(1)} %get-tuple-element.187, f32[4,384]{1,0:T(4,128)S(1)} %get-tuple-element.278, ...), kind=kOutput, calls=%fused_computation.11 | convolution fusion | flops 307101696 | bytes 6795268 | tf_op jit(solution)/shard_map/while/body/eval_jaxpr/cond/branch_1_fun/hqk,kd->hqd/dot_general | solution.py:37
  91.0 0.6 dynamic_slice.36
  91.5 1.2 iota_add_fusion.3
  94.0 6.4 %conditional.2 = ((f32[4,384]{1,0:T(4,128)S(1)}, f32[4,384]{1,0:T(4,128)S(1)}, f32[4,384,128]{2,1,0:T(8,128)S(1)})) conditional(s32[]{:T(128)} %convert_element_type.31, (f32[4,384]{1,0:T(4,128)S(1)}, f32[4,384]{1,0:T(4,128)S(1)}, f32[4,384,128]{2,1,0:T(8,128)S(1)}) %tuple.53, (s32[768]{0:T(1024)S(1)}, s32[384]{0:T(512)S(1)}, s32[]{:T(128)}, ...), branch_computations={%region_6.7_spmd, %region_7.10_spmd} | conditional | flops 617647104 | bytes 17797706 | solution.py:58
  95.6 0.2 broadcast_compare_fusion
  95.9 1.0 fusion
  96.9 1.0 fusion.4
  97.9 2.5 %fusion.8 = f32[4,384,128]{2,1,0:T(8,128)S(1)} fusion(f32[768,384,4]{1,0,2:T(8,128)S(1)} %get-tuple-element.282, f32[4,384]{1,0:T(4,128)S(1)} %max.5, pred[384,768]{0,1:T(8,128)(4,1)S(1)} %broadcast_compare_fusion, f32[4,384,128]{2,1,0:T(8,128)S(1)} %get-tuple-element.187, f32[4,384]{1,0:T(4,128)S(1)} %get-tuple-element.278, ...), kind=kOutput, calls=%fused_computation.11 | convolution fusion | flops 307101696 | bytes 6795268 | tf_op jit(solution)/shard_map/while/body/eval_jaxpr/cond/branch_1_fun/hqk,kd->hqd/dot_general | solution.py:37
  100.4 0.6 dynamic_slice.36
  101.0 1.2 iota_add_fusion.3
  103.4 6.4 %conditional.2 = ((f32[4,384]{1,0:T(4,128)S(1)}, f32[4,384]{1,0:T(4,128)S(1)}, f32[4,384,128]{2,1,0:T(8,128)S(1)})) conditional(s32[]{:T(128)} %convert_element_type.31, (f32[4,384]{1,0:T(4,128)S(1)}, f32[4,384]{1,0:T(4,128)S(1)}, f32[4,384,128]{2,1,0:T(8,128)S(1)}) %tuple.53, (s32[768]{0:T(1024)S(1)}, s32[384]{0:T(512)S(1)}, s32[]{:T(128)}, ...), branch_computations={%region_6.7_spmd, %region_7.10_spmd} | conditional | flops 617647104 | bytes 17797706 | solution.py:58
  105.1 0.2 broadcast_compare_fusion
  105.3 1.0 fusion
  106.3 1.0 fusion.4
  107.3 2.5 %fusion.8 = f32[4,384,128]{2,1,0:T(8,128)S(1)} fusion(f32[768,384,4]{1,0,2:T(8,128)S(1)} %get-tuple-element.282, f32[4,384]{1,0:T(4,128)S(1)} %max.5, pred[384,768]{0,1:T(8,128)(4,1)S(1)} %broadcast_compare_fusion, f32[4,384,128]{2,1,0:T(8,128)S(1)} %get-tuple-element.187, f32[4,384]{1,0:T(4,128)S(1)} %get-tuple-element.278, ...), kind=kOutput, calls=%fused_computation.11 | convolution fusion | flops 307101696 | bytes 6795268 | tf_op jit(solution)/shard_map/while/body/eval_jaxpr/cond/branch_1_fun/hqk,kd->hqd/dot_general | solution.py:37
  109.8 0.3 fusion.21
  110.1 0.3 copy.48
  110.4 0.2 convert_element_type.22
  110.6 13.6 %all_to_all.64 = bf16[4,96,512]{2,1,0:T(8,128)(2,1)S(1)} all-to-all(bf16[4,96,512]{2,1,0:T(8,128)(2,1)S(1)} %convert_element_type.22), channel_id=1, replica_groups=mesh['cp'=8,'sp'=4] {'sp'}, dimensions={0} | all-to-all | bytes 786432 | tf_op jit(solution)/shard_map/all_to_all | solution.py:153
  124.2 0.8 copy.52
  (21 shorter events, 0.2 us)
Async XLA Ops:
  0.0 25.2 %copy-start = (bf16[96,512]{1,0:T(8,128)(2,1)S(1)}, bf16[96,512]{1,0:T(8,128)(2,1)}, u32[]{:S(2)}) copy-start(bf16[96,512]{1,0:T(8,128)(2,1)} %param.12) | copy-start | bytes 294916
  0.0 36.4 %copy-start.1 = (s32[8]{0:T(128)S(1)}, s32[8]{0:T(128)}, u32[]{:S(2)}) copy-start(s32[8]{0:T(128)} %param.13) | copy-start | bytes 100
  1.8 18.3 %all-to-all-start.1 = ((bf16[96,4,512]{2,0,1:T(8,128)(2,1)}), bf16[96,4,512]{2,0,1:T(8,128)(2,1)S(1)}, u32[]{:S(2)}, u32[]{:S(2)}) async-start(bf16[96,4,512]{2,0,1:T(8,128)(2,1)} %bitcast.49), calls=%async_computation.1 | async-start | bytes 786432 | tf_op jit(solution)/shard_map/all_to_all | solution.py:84
  20.1 25.7 %all-to-all-start = ((bf16[768,4,128]{0,2,1:T(8,128)(2,1)}), bf16[768,4,128]{0,2,1:T(8,128)(2,1)S(1)}, u32[]{:S(2)}, u32[]{:S(2)}) async-start(bf16[768,4,128]{0,2,1:T(8,128)(2,1)} %bitcast.4), calls=%async_computation | async-start | bytes 1572864 | tf_op jit(solution)/shard_map/all_to_all | solution.py:108
  45.8 23.2 %all-to-all-start.2 = ((bf16[768,4,128]{0,2,1:T(8,128)(2,1)}), bf16[768,4,128]{0,2,1:T(8,128)(2,1)S(1)}, u32[]{:S(2)}, u32[]{:S(2)}) async-start(bf16[768,4,128]{0,2,1:T(8,128)(2,1)} %bitcast.11), calls=%async_computation.2 | async-start | bytes 1572864 | tf_op jit(solution)/shard_map/all_to_all | solution.py:109
where the time goes:
time: 124 us; the launch traced here: 125 us
  blocking collectives  34.4 us (28%)
  waiting for transfers between devices  27.5 us (22%)
  starting transfers between devices  14.9 us (12%)
  matrix products  13.7 us (11%)
  other arithmetic  12.2 us (10%)
  loops' own time  12 us (10%)
  local copies, waits for them, and re-layouts  10.1 us (8%)
    all_to_all x1, waiting for transfers between devices, per_device(): lax.all_to_all(whole_value, 'sp', split_axis=1, concat_axis=0, tiled=True)  18.2 us
    all_to_all x1, blocking collectives, per_device(): lax.all_to_all(mixed_rows, 'sp', split_axis=0, concat_axis=1, tiled=True)  13.6 us
    all_gather x1, blocking collectives, per_device(): lax.all_gather(key_vectors, 'cp', axis=0, tiled=True)  10.7 us
    all_gather x1, blocking collectives, per_device(): lax.all_gather(value_matrix, 'cp', axis=0, tiled=True)  10 us
    dot_general x4, matrix products, absorb_block(): jnp.einsum('hqk,kd->hqd', weights.astype(jnp.bfloat16), value_blk, prefer...  9.88 us
    all_to_all x1, waiting for transfers between devices, per_device(): lax.all_to_all(whole_key, 'sp', split_axis=1, concat_axis=0, tiled=True)  9.34 us
    another operation x4, loops' own time, guarded(): return lax.cond(lowest <= jnp.max(query_pos), compute, unchanged, state_in)  6.78 us
    all_to_all x1, starting transfers between devices, per_device(): lax.all_to_all(queries, 'sp', split_axis=1, concat_axis=0, tiled=True)  6.35 us
  transfers between devices with their start and end apart: 3, of which 2 were waited for; matrix products, arithmetic and copies ran while one was open for 3% of the time, Pallas kernels for 0%

commit v1 on v0

v1 whole, which is shorter than its diff:
```python
import functools
import math

import jax
import jax.numpy as jnp
from jax import lax
from jax.experimental import pallas as pl
from jax.experimental.pallas import tpu as pltpu
from jax.sharding import PartitionSpec as P

HEAD_WIDTH = 128
MASKED = -1e30
MESH = pl.DeviceIdType.MESH


def forward_dims(kind, offset, dims):
    order = list(range(1, dims)) + [0] if kind == 0 else list(range(dims - 1, 0, -1)) + [0]
    last = max([order.index(b) for b in range(dims) if offset >> b & 1], default=-1)
    return order[last + 1 :]


def body(cp, sp, order_ref, q_ref, k_ref, v_ref, out_ref,
         qbuf, kbuf, vbuf, obuf, acc_e, acc_l,
         local_sem, zsend, zrecv, qsend, qrecv, csend, crecv, osend, orecv):
    dims = cp.bit_length() - 1
    c = lax.axis_index("cp")
    s = lax.axis_index("sp")
    tok = k_ref.shape[0]
    span = tok * sp // 2
    qcols = q_ref.shape[1] // sp
    heads = qcols // HEAD_WIDTH
    width = heads * span
    kv_src = (k_ref, v_ref)
    kv_buf = (kbuf, vbuf)

    peers = [(c, s ^ k) for k in range(1, sp)] + [(c ^ (1 << d), s) for d in range(dims)]
    barrier = pltpu.get_barrier_semaphore()
    for peer in peers:
        pl.semaphore_signal(barrier, inc=1, device_id=peer, device_id_type=MESH)

    def columns(index, size):
        return pl.ds(pl.multiple_of(index * size, size), size)

    def rows(index):
        return pl.ds(pl.multiple_of(index * tok, tok), tok)

    own = []
    for kind in range(2):
        own.append(pltpu.make_async_copy(
            kv_src[kind].at[:, columns(s, HEAD_WIDTH)],
            kv_buf[kind].at[c, rows(s), :], local_sem.at[kind]))
    own.append(pltpu.make_async_copy(q_ref.at[:, columns(s, qcols)], qbuf.at[s], local_sem.at[2]))
    for copy in own:
        copy.start()
    pl.semaphore_wait(barrier, len(peers))

    far_first = [k for k in range(sp // 2, sp)] + [k for k in range(1, sp // 2)]
    sends = []
    for k in far_first:
        for kind in range(2):
            copy = pltpu.make_async_remote_copy(
                src_ref=kv_src[kind].at[:, columns(s ^ k, HEAD_WIDTH)],
                dst_ref=kv_buf[kind].at[c, rows(s), :],
                send_sem=zsend.at[kind, k], recv_sem=zrecv.at[kind, k],
                device_id=(c, s ^ k), device_id_type=MESH)
            copy.start()
            sends.append(copy)
    q_copies = {}
    for k in far_first:
        copy = pltpu.make_async_remote_copy(
            src_ref=q_ref.at[:, columns(s ^ k, qcols)], dst_ref=qbuf.at[s],
            send_sem=qsend.at[k], recv_sem=qrecv.at[k],
            device_id=(c, s ^ k), device_id_type=MESH)
        copy.start()
        sends.append(copy)
        q_copies[k] = copy

    def z_wait(kind, k):
        piece = kv_buf[kind].at[c, rows(s ^ k), :]
        pltpu.make_async_remote_copy(
            src_ref=piece, dst_ref=piece, send_sem=zsend.at[kind, k], recv_sem=zrecv.at[kind, k],
            device_id=(c, s ^ k), device_id_type=MESH).wait_recv()

    def c_copy(kind, offset, k, dim):
        piece = kv_buf[kind].at[c ^ offset, rows(s ^ k), :]
        return pltpu.make_async_remote_copy(
            src_ref=piece, dst_ref=piece,
            send_sem=csend.at[kind, offset, k, dim],
            recv_sem=crecv.at[kind, offset ^ (1 << dim), k],
            device_id=(c ^ (1 << dim), s), device_id_type=MESH)

    def c_wait(kind, offset, k):
        piece = kv_buf[kind].at[c ^ offset, rows(s ^ k), :]
        pltpu.make_async_remote_copy(
            src_ref=piece, dst_ref=piece,
            send_sem=csend.at[kind, 0, k, 0], recv_sem=crecv.at[kind, offset, k],
            device_id=(c ^ 1, s), device_id_type=MESH).wait_recv()

    arrival = [0] + far_first
    events = []
    for offset in range(cp):
        for rank, k in enumerate(arrival):
            events.append((rank + 2 * bin(offset >> 1).count("1") + (offset & 1), offset & 1, offset, k))
    events.sort()
    for _, _, offset, k in events:
        for kind in range(2):
            if offset:
                c_wait(kind, offset, k)
            elif k:
                z_wait(kind, k)
            else:
                own[kind].wait()
            for dim in forward_dims(kind, offset, dims):
                copy = c_copy(kind, offset, k, dim)
                copy.start()
                sends.append(copy)
    own[2].wait()
    for k in far_first:
        q_copies[k].wait_recv()

    factor = math.log2(math.e) / math.sqrt(HEAD_WIDTH)
    half = sp // 2

    def gather_q(first):
        parts = []
        for h in range(heads):
            for j in range(half):
                parts.append(qbuf[first + j, :, h * HEAD_WIDTH : (h + 1) * HEAD_WIDTH])
        return jnp.concatenate(parts, axis=0).T

    qe = gather_q(0)
    ql = gather_q(half)

    def scores(key, query):
        return jnp.dot(key, query, preferred_element_type=jnp.float32)

    def peak(x):
        return jnp.max(x, axis=0, keepdims=True)

    def total(x):
        return jnp.sum(x, axis=0, keepdims=True)

    def weigh(x, top):
        return jnp.exp2(x * factor - top * factor)

    def mix(value, weights):
        return lax.dot_general(value, weights.astype(jnp.bfloat16), (((0,), (0,)), ((), ())),
                               preferred_element_type=jnp.float32)

    early = order_ref[c]
    key_e, key_l = kbuf[c, :span, :], kbuf[c, span:, :]
    val_e, val_l = vbuf[c, :span, :], vbuf[c, span:, :]
    allowed = lax.broadcasted_iota(jnp.int32, (span, width), 0) <= (
        lax.broadcasted_iota(jnp.int32, (span, width), 1) % span)
    x = jnp.where(allowed, scores(key_e, qe), MASKED)
    me = peak(x)
    w = weigh(x, me)
    le = total(w)
    acc_e[...] = mix(val_e, w)
    x1 = scores(key_e, ql)
    x2 = jnp.where(allowed, scores(key_l, ql), MASKED)
    ml = jnp.maximum(peak(x1), peak(x2))
    w1 = weigh(x1, ml)
    w2 = weigh(x2, ml)
    ll = total(w1) + total(w2)
    acc_l[...] = mix(val_e, w1) + mix(val_l, w2)

    def step(offset, state):
        me, le, ml, ll = state
        other = c ^ offset
        first = order_ref[other] < early
        key_e, key_l = kbuf[other, :span, :], kbuf[other, span:, :]
        val_e, val_l = vbuf[other, :span, :], vbuf[other, span:, :]
        x1 = scores(key_e, ql)
        x2 = scores(jnp.where(first, key_e, key_l), jnp.where(first, qe, ql))
        p1, p2 = peak(x1), peak(x2)
        new_l = jnp.maximum(jnp.maximum(ml, p1), jnp.where(first, ml, p2))
        new_e = jnp.where(first, jnp.maximum(me, p2), me)
        w1 = weigh(x1, new_l)
        w2 = weigh(x2, jnp.where(first, new_e, new_l))
        fe = jnp.exp2((me - new_e) * factor)
        fl = jnp.exp2((ml - new_l) * factor)
        t2 = total(w2)
        le = le * fe + jnp.where(first, t2, 0.0)
        ll = ll * fl + total(w1) + jnp.where(first, 0.0, t2)
        d1 = mix(val_e, w1)
        d2 = mix(jnp.where(first, val_e, val_l), w2)
        acc_e[...] = acc_e[...] * fe + jnp.where(first, d2, 0.0)
        acc_l[...] = acc_l[...] * fl + d1 + jnp.where(first, 0.0, d2)
        return (new_e, le, new_l, ll)

    me, le, ml, ll = lax.fori_loop(1, cp, step, (me, le, ml, ll))

    for first, acc, norm in ((0, acc_e, le), (half, acc_l, ll)):
        done = (acc[...] / norm).T.astype(jnp.bfloat16)
        for h in range(heads):
            for j in range(half):
                start = h * span + j * tok
                obuf[first + j, :, h * HEAD_WIDTH : (h + 1) * HEAD_WIDTH] = done[start : start + tok, :]
    last = pltpu.make_async_copy(obuf.at[s], out_ref.at[:, columns(s, qcols)], local_sem.at[3])
    last.start()
    o_copies = []
    for k in far_first:
        copy = pltpu.make_async_remote_copy(
            src_ref=obuf.at[s ^ k], dst_ref=out_ref.at[:, columns(s, qcols)],
            send_sem=osend.at[k], recv_sem=orecv.at[k],
            device_id=(c, s ^ k), device_id_type=MESH)
        copy.start()
        o_copies.append(copy)
    last.wait()
    for copy in o_copies:
        copy.wait()
    for copy in sends:
        copy.wait_send()


def per_device(queries, key_vectors, value_matrix, span_order):
    cp = lax.axis_size("cp")
    sp = lax.axis_size("sp")
    tok, q_width = queries.shape
    group = tok * sp
    qcols = q_width // sp
    width = qcols // HEAD_WIDTH * (group // 2)
    dims = cp.bit_length() - 1
    vmem = pl.BlockSpec(memory_space=pltpu.VMEM)
    dma = pltpu.SemaphoreType.DMA
    return pl.pallas_call(
        functools.partial(body, cp, sp),
        out_shape=jax.ShapeDtypeStruct((tok, q_width), jnp.bfloat16),
        in_specs=[pl.BlockSpec(memory_space=pltpu.SMEM), vmem, vmem, vmem],
        out_specs=vmem,
        scratch_shapes=[
            pltpu.VMEM((sp, tok, qcols), jnp.bfloat16),
            pltpu.VMEM((cp, group, HEAD_WIDTH), jnp.bfloat16),
            pltpu.VMEM((cp, group, HEAD_WIDTH), jnp.bfloat16),
            pltpu.VMEM((sp, tok, qcols), jnp.bfloat16),
            pltpu.VMEM((HEAD_WIDTH, width), jnp.float32),
            pltpu.VMEM((HEAD_WIDTH, width), jnp.float32),
            dma((4,)), dma((2, sp)), dma((2, sp)), dma((sp,)), dma((sp,)),
            dma((2, cp, sp, dims)), dma((2, cp, sp)), dma((sp,)), dma((sp,)),
        ],
        compiler_params=pltpu.CompilerParams(
            collective_id=0, has_side_effects=True, vmem_limit_bytes=60 * 1024 * 1024),
    )(span_order, queries, key_vectors, value_matrix)


def solution(mesh):
    return jax.shard_map(
        per_device,
        mesh=mesh,
        in_specs=(P(("cp", "sp"), None), P(("cp", "sp"), None), P(("cp", "sp"), None), P()),
        out_specs=P(("cp", "sp"), None),
        check_vma=False,
    )
```

time: 124 us -> 45.4 us (0.37)
  Pallas kernels: 0 us -> 43.5 us
  blocking collectives: 34.4 us -> 0 us
  waiting for transfers between devices: 27.5 us -> 0 us
  starting transfers between devices: 14.9 us -> 0 us
  matrix products: 13.7 us -> 0 us
  other arithmetic: 12.2 us -> 0 us
  loops' own time: 12 us -> 0 us
  local copies, waits for them, and re-layouts: 10.1 us -> 1.77 us
    pallas_call x0 -> x1, Pallas kernels: none -> 43.5 us  [per_device(): pl.pallas_call(functools.partial(body, cp, sp), out_shape=jax.ShapeDtypeS...]
    all_to_all x3 -> x0, waiting for transfers between devices: 27.5 us -> none  [the longest x1 18.2 us: per_device(): lax.all_to_all(whole_value, 'sp', split_axis=1, concat_axis=0, tiled=True)]
    all_gather x2 -> x0, blocking collectives: 20.7 us -> none  [the longest x1 10.7 us: per_device(): lax.all_gather(key_vectors, 'cp', axis=0, tiled=True)]
    all_to_all x3 -> x0, starting transfers between devices: 14.9 us -> none  [the longest x1 6.35 us: per_device(): lax.all_to_all(queries, 'sp', split_axis=1, concat_axis=0, tiled=True)]
    dot_general x8 -> x0, matrix products: 13.7 us -> none  [the longest x4 9.88 us: absorb_block(): jnp.einsum('hqk,kd->hqd', weights.astype(jnp.bfloat16), value_blk, prefer...]
    all_to_all x1 -> x0, blocking collectives: 13.6 us -> none  [per_device(): lax.all_to_all(mixed_rows, 'sp', split_axis=0, concat_axis=1, tiled=True)]
    another operation x5 -> x0, loops' own time: 12 us -> none  [the longest x4 6.78 us: guarded(): return lax.cond(lowest <= jnp.max(query_pos), compute, unchanged, state_in)]
    add x8 -> x0, other arithmetic: 4.87 us -> none  [the longest x4 4.8 us: advance(): key_pos = position_of(offset + jnp.arange(block_row_list, dtype=jnp.int32))]
  transfers between devices with their start and end apart: 3 -> 0, of which waited for: 2 -> 0; matrix products, arithmetic and copies ran while one was open for 3% -> 0% of each run, Pallas kernels for 0% -> 0%
where the time goes in v1:
time: 45.4 us; the launch traced here: 45.3 us
  Pallas kernels  43.5 us (96%)
  local copies, waits for them, and re-layouts  1.77 us (4%)
    pallas_call x1, Pallas kernels, per_device(): pl.pallas_call(functools.partial(body, cp, sp), out_shape=jax.ShapeDtypeS...  43.5 us
    unnamed x1, local copies, waits for them, and re-layouts  1.77 us

profile of v1, /device:TPU:0, one launch (start us, length us, event | category | flops | bytes accessed | tf_op | source)
XLA Modules:
  0.0 45.3 jit_solution(11236955839597616666)
XLA Ops:
  0.0 43.5 %shard_map.46 = bf16[96,2048]{1,0:T(8,128)(2,1)} custom-call(s32[8]{0:T(128)} %order_ref.1, bf16[96,2048]{1,0:T(8,128)(2,1)} %q_ref.1, bf16[96,512]{1,0:T(8,128)(2,1)} %k_ref.1, bf16[96,512]{1,0:T(8,128)(2,1)} %v_ref.1), custom_call_target="tpu_custom_call" | custom-call | tf_op jit(solution)/shard_map/pallas_call | solution.py:227
  43.5 1.8 %copy.6 = bf16[96,2048]{1,0:T(8,128)(2,1)} copy(bf16[96,2048]{1,0:T(8,128)(2,1)} %shard_map.46) | data formatting | bytes 786432

commit v2 on v1

v2 whole, which is shorter than its diff:
```python
import functools
import math

import jax
import jax.numpy as jnp
from jax import lax
from jax.experimental import pallas as pl
from jax.experimental.pallas import tpu as pltpu
from jax.sharding import PartitionSpec as P

HEAD_WIDTH = 128
MASKED = -1e30
CHUNKS = 2
QUERY_AT = 8
UNROLL = 7
MESH = pl.DeviceIdType.MESH


def forward_dims(kind, offset, dims):
    order = list(range(1, dims)) + [0] if kind == 0 else list(range(dims - 1, 0, -1)) + [0]
    last = max([order.index(b) for b in range(dims) if offset >> b & 1], default=-1)
    return order[last + 1 :]


def body(cp, sp, order_ref, q_ref, k_ref, v_ref, out_ref,
         qbuf, kbuf, vbuf, obuf, acc_e, acc_l,
         local_sem, zsend, zrecv, qsend, qrecv, csend, crecv, osend, orecv):
    dims = cp.bit_length() - 1
    c = lax.axis_index("cp")
    s = lax.axis_index("sp")
    tok = k_ref.shape[0]
    span = tok * sp // 2
    qcols = q_ref.shape[1] // sp
    heads = qcols // HEAD_WIDTH
    chunks = CHUNKS
    ccols = qcols // chunks
    heads = heads // chunks
    width = heads * span
    kv_src = (k_ref, v_ref)
    kv_buf = (kbuf, vbuf)

    peers = [(c, s ^ k) for k in range(1, sp)] + [(c ^ (1 << d), s) for d in range(dims)]
    barrier = pltpu.get_barrier_semaphore()
    for peer in peers:
        pl.semaphore_signal(barrier, inc=1, device_id=peer, device_id_type=MESH)

    def columns(index, size):
        return pl.ds(pl.multiple_of(index * size, size), size)

    def rows(index):
        return pl.ds(pl.multiple_of(index * tok, tok), tok)

    own = []
    for kind in range(2):
        own.append(pltpu.make_async_copy(
            kv_src[kind].at[:, columns(s, HEAD_WIDTH)],
            kv_buf[kind].at[c, rows(s), :], local_sem.at[kind]))
    for chunk in range(chunks):
        own.append(pltpu.make_async_copy(
            q_ref.at[:, columns(s * chunks + chunk, ccols)], qbuf.at[chunk, s],
            local_sem.at[2 + chunk]))
    for copy in own:
        copy.start()
    pl.semaphore_wait(barrier, len(peers))

    far_first = [k for k in range(sp // 2, sp)] + [k for k in range(1, sp // 2)]
    sends = []
    for k in far_first:
        for kind in range(2):
            copy = pltpu.make_async_remote_copy(
                src_ref=kv_src[kind].at[:, columns(s ^ k, HEAD_WIDTH)],
                dst_ref=kv_buf[kind].at[c, rows(s), :],
                send_sem=zsend.at[kind, k], recv_sem=zrecv.at[kind, k],
                device_id=(c, s ^ k), device_id_type=MESH)
            copy.start()
            sends.append(copy)
    q_copies = []

    def send_queries():
        for chunk in range(chunks):
            for k in far_first:
                copy = pltpu.make_async_remote_copy(
                    src_ref=q_ref.at[:, columns((s ^ k) * chunks + chunk, ccols)],
                    dst_ref=qbuf.at[chunk, s],
                    send_sem=qsend.at[chunk, k], recv_sem=qrecv.at[chunk, k],
                    device_id=(c, s ^ k), device_id_type=MESH)
                copy.start()
                sends.append(copy)
                q_copies.append((chunk, copy))


    def z_wait(kind, k):
        piece = kv_buf[kind].at[c, rows(s ^ k), :]
        pltpu.make_async_remote_copy(
            src_ref=piece, dst_ref=piece, send_sem=zsend.at[kind, k], recv_sem=zrecv.at[kind, k],
            device_id=(c, s ^ k), device_id_type=MESH).wait_recv()

    def c_copy(kind, offset, k, dim):
        piece = kv_buf[kind].at[c ^ offset, rows(s ^ k), :]
        return pltpu.make_async_remote_copy(
            src_ref=piece, dst_ref=piece,
            send_sem=csend.at[kind, offset, k, dim],
            recv_sem=crecv.at[kind, offset ^ (1 << dim), k],
            device_id=(c ^ (1 << dim), s), device_id_type=MESH)

    def c_wait(kind, offset, k):
        piece = kv_buf[kind].at[c ^ offset, rows(s ^ k), :]
        pltpu.make_async_remote_copy(
            src_ref=piece, dst_ref=piece,
            send_sem=csend.at[kind, 0, k, 0], recv_sem=crecv.at[kind, offset, k],
            device_id=(c ^ 1, s), device_id_type=MESH).wait_recv()

    arrival = [0] + far_first
    events = []
    for offset in range(cp):
        for rank, k in enumerate(arrival):
            events.append((rank + 2 * bin(offset >> 1).count("1") + (offset & 1), offset & 1, offset, k))
    events.sort()
    for index, (_, _, offset, k) in enumerate(events):
        if index == min(QUERY_AT, len(events) - 1):
            send_queries()
        for kind in range(2):
            if offset:
                c_wait(kind, offset, k)
            elif k:
                z_wait(kind, k)
            else:
                own[kind].wait()
            for dim in forward_dims(kind, offset, dims):
                copy = c_copy(kind, offset, k, dim)
                copy.start()
                sends.append(copy)

    factor = math.log2(math.e) / math.sqrt(HEAD_WIDTH)
    half = sp // 2

    def gather_q(chunk, first):
        parts = []
        for h in range(heads):
            for j in range(half):
                parts.append(qbuf[chunk, first + j, :, h * HEAD_WIDTH : (h + 1) * HEAD_WIDTH])
        return jnp.concatenate(parts, axis=0).T

    def scores(key, query):
        return jnp.dot(key, query, preferred_element_type=jnp.float32)

    def peak(x):
        return jnp.max(x, axis=0, keepdims=True)

    def total(x):
        return jnp.sum(x, axis=0, keepdims=True)

    def weigh(x, top):
        return jnp.exp2(x * factor - top * factor)

    def mix(value, weights):
        return lax.dot_general(value, weights.astype(jnp.bfloat16), (((0,), (0,)), ((), ())),
                               preferred_element_type=jnp.float32)

    early = order_ref[c]
    key_e, key_l = kbuf[c, :span, :], kbuf[c, span:, :]
    val_e, val_l = vbuf[c, :span, :], vbuf[c, span:, :]
    allowed = lax.broadcasted_iota(jnp.int32, (span, width), 0) <= (
        lax.broadcasted_iota(jnp.int32, (span, width), 1) % span)

    def attend(chunk):
        qe = gather_q(chunk, 0)
        ql = gather_q(chunk, half)
        x = jnp.where(allowed, scores(key_e, qe), MASKED)
        me = peak(x)
        w = weigh(x, me)
        le = total(w)
        acc_e[...] = mix(val_e, w)
        x1 = scores(key_e, ql)
        x2 = jnp.where(allowed, scores(key_l, ql), MASKED)
        ml = jnp.maximum(peak(x1), peak(x2))
        w1 = weigh(x1, ml)
        w2 = weigh(x2, ml)
        ll = total(w1) + total(w2)
        acc_l[...] = mix(val_e, w1) + mix(val_l, w2)

        def step(offset, state):
            me, le, ml, ll = state
            other = c ^ offset
            first = order_ref[other] < early
            key_e, key_l = kbuf[other, :span, :], kbuf[other, span:, :]
            val_e, val_l = vbuf[other, :span, :], vbuf[other, span:, :]
            x1 = scores(key_e, ql)
            x2 = scores(jnp.where(first, key_e, key_l), jnp.where(first, qe, ql))
            p1, p2 = peak(x1), peak(x2)
            new_l = jnp.maximum(jnp.maximum(ml, p1), jnp.where(first, ml, p2))
            new_e = jnp.where(first, jnp.maximum(me, p2), me)
            w1 = weigh(x1, new_l)
            w2 = weigh(x2, jnp.where(first, new_e, new_l))
            fe = jnp.exp2((me - new_e) * factor)
            fl = jnp.exp2((ml - new_l) * factor)
            t2 = total(w2)
            le = le * fe + jnp.where(first, t2, 0.0)
            ll = ll * fl + total(w1) + jnp.where(first, 0.0, t2)
            d1 = mix(val_e, w1)
            d2 = mix(jnp.where(first, val_e, val_l), w2)
            acc_e[...] = acc_e[...] * fe + jnp.where(first, d2, 0.0)
            acc_l[...] = acc_l[...] * fl + d1 + jnp.where(first, 0.0, d2)
            return (new_e, le, new_l, ll)

        me, le, ml, ll = lax.fori_loop(1, cp, step, (me, le, ml, ll), unroll=UNROLL)

        for first, acc, norm in ((0, acc_e, le), (half, acc_l, ll)):
            done = (acc[...] / norm).T.astype(jnp.bfloat16)
            for h in range(heads):
                for j in range(half):
                    start = h * span + j * tok
                    obuf[chunk, first + j, :, h * HEAD_WIDTH : (h + 1) * HEAD_WIDTH] = done[start : start + tok, :]

    outs = []
    for chunk in range(chunks):
        own[2 + chunk].wait()
        for which, copy in q_copies:
            if which == chunk:
                copy.wait_recv()
        attend(chunk)
        place = columns(s * chunks + chunk, ccols)
        last = pltpu.make_async_copy(
            obuf.at[chunk, s], out_ref.at[:, place], local_sem.at[2 + chunks + chunk])
        last.start()
        outs.append(last)
        for k in far_first:
            copy = pltpu.make_async_remote_copy(
                src_ref=obuf.at[chunk, s ^ k], dst_ref=out_ref.at[:, place],
                send_sem=osend.at[chunk, k], recv_sem=orecv.at[chunk, k],
                device_id=(c, s ^ k), device_id_type=MESH)
            copy.start()
            outs.append(copy)
    for copy in outs:
        copy.wait()
    for copy in sends:
        copy.wait_send()


def per_device(queries, key_vectors, value_matrix, span_order):
    cp = lax.axis_size("cp")
    sp = lax.axis_size("sp")
    tok, q_width = queries.shape
    group = tok * sp
    qcols = q_width // sp
    width = qcols // HEAD_WIDTH // CHUNKS * (group // 2)
    dims = cp.bit_length() - 1
    anywhere = pl.BlockSpec(memory_space=pl.ANY)
    dma = pltpu.SemaphoreType.DMA
    return pl.pallas_call(
        functools.partial(body, cp, sp),
        out_shape=jax.ShapeDtypeStruct((tok, q_width), jnp.bfloat16),
        in_specs=[pl.BlockSpec(memory_space=pltpu.SMEM)] + [anywhere] * 3,
        out_specs=anywhere,
        scratch_shapes=[
            pltpu.VMEM((CHUNKS, sp, tok, qcols // CHUNKS), jnp.bfloat16),
            pltpu.VMEM((cp, group, HEAD_WIDTH), jnp.bfloat16),
            pltpu.VMEM((cp, group, HEAD_WIDTH), jnp.bfloat16),
            pltpu.VMEM((CHUNKS, sp, tok, qcols // CHUNKS), jnp.bfloat16),
            pltpu.VMEM((HEAD_WIDTH, width), jnp.float32),
            pltpu.VMEM((HEAD_WIDTH, width), jnp.float32),
            dma((2 + 2 * CHUNKS,)), dma((2, sp)), dma((2, sp)), dma((CHUNKS, sp)), dma((CHUNKS, sp)),
            dma((2, cp, sp, dims)), dma((2, cp, sp)), dma((CHUNKS, sp)), dma((CHUNKS, sp)),
        ],
        compiler_params=pltpu.CompilerParams(
            collective_id=0, has_side_effects=True, vmem_limit_bytes=60 * 1024 * 1024),
    )(span_order, queries, key_vectors, value_matrix)


def solution(mesh):
    return jax.shard_map(
        per_device,
        mesh=mesh,
        in_specs=(P(("cp", "sp"), None), P(("cp", "sp"), None), P(("cp", "sp"), None), P()),
        out_specs=P(("cp", "sp"), None),
        check_vma=False,
    )
```

time: 45.4 us -> 38.6 us (0.85)
  Pallas kernels: 43.5 us -> 36.7 us
    pallas_call x1, Pallas kernels: 43.5 us -> 36.7 us  [per_device(): pl.pallas_call(functools.partial(body, cp, sp), out_shape=jax.ShapeDtypeS...]
where the time goes in v2:
time: 38.6 us; the launch traced here: 38.5 us
  Pallas kernels  36.7 us (95%)
  local copies, waits for them, and re-layouts  1.77 us (5%)
    pallas_call x1, Pallas kernels, per_device(): pl.pallas_call(functools.partial(body, cp, sp), out_shape=jax.ShapeDtypeS...  36.7 us
    unnamed x1, local copies, waits for them, and re-layouts  1.77 us

profile of v2, /device:TPU:0, one launch (start us, length us, event | category | flops | bytes accessed | tf_op | source)
XLA Modules:
  0.0 38.5 jit_solution(11634337459582500617)
XLA Ops:
  0.0 36.7 %shard_map.46 = bf16[96,2048]{1,0:T(8,128)(2,1)} custom-call(s32[8]{0:T(128)} %order_ref.1, bf16[96,2048]{1,0:T(8,128)(2,1)} %q_ref.1, bf16[96,512]{1,0:T(8,128)(2,1)} %k_ref.1, bf16[96,512]{1,0:T(8,128)(2,1)} %v_ref.1), custom_call_target="tpu_custom_call" | custom-call | tf_op jit(solution)/shard_map/pallas_call | solution.py:250
  36.7 1.8 %copy.6 = bf16[96,2048]{1,0:T(8,128)(2,1)} copy(bf16[96,2048]{1,0:T(8,128)(2,1)} %shard_map.46) | data formatting | bytes 786432
